TPU v7x, 512 devices: a whole 4x4x16 slice. The times are simulated.
512 devices in a mesh: seq: 64 (over y, z), fsdp: 8 (over x, core).
Axes of the slice: x: 4, y: 4, z: 16, core: 2. Of those that a mesh axis runs over, the one named last changes fastest.
Arguments:
- probe_tensor: bfloat16 [8192, 8, 2048], P('seq', 'fsdp'), may hold values from -10 to 10
- matcher_tensor: bfloat16 [8192, 8, 2048], P('seq', 'fsdp'), may hold values from -10 to 10
- payload_tensor: bfloat16 [8192, 8, 2048], P('seq', 'fsdp'), may hold values from -6 to 6
- adjoint_attended: bfloat16 [8192, 8, 2048], P('seq', 'fsdp'), may hold values from -6 to 6
- logit_scale: float32 [16], replicated, may hold values from 0.5 to 2
- anchor_tiles: int32 [16, 2], replicated, may hold values from 0 to 127, as said below
- sampled_tiles: int32 [16, 128, 3], replicated, may hold values from 0 to 127, as said below
Outputs:
- query_gradients: bfloat16 [8192, 8, 2048], P('seq', 'fsdp')
- grad_key: bfloat16 [8192, 8, 2048], P('seq', 'fsdp')
- grad_value: bfloat16 [8192, 8, 2048], P('seq', 'fsdp')
- adjoint_scales: float32 [16], replicated
Inputs may be any that keep to these rules, and one draw needn't show every extreme that they name: `anchor_tiles`: each head lists 2 different blocks. `sampled_tiles`: each row lists 3 different blocks, none within one block of the row's own block and none among the head's global blocks.
All inputs are finite; a program needn't handle non-finite values.
Results may differ from a plain program's by a relative error of at most 0.0083.
Values may be sent and summed in bfloat16 or wider, within the bound.
No kernel may reach another device: no remote copies, remote signals or barrier semaphores. Data moves between devices by JAX's collectives and lax.ppermute only.
A program may use at most 64 MiB of HBM per device.

v0:
```python
import math

import jax
import jax.numpy as jnp
from jax import lax
from jax.sharding import PartitionSpec as P

TILE_SPAN = 64


masked_minimum = -1e30


def group_of():
    for size in (8, 4, 2):
        return size
    return 1


def block_lists(anchor_tiles, sampled_tiles, nblocks):
    channel_roster = anchor_tiles.shape[0]
    block_ids = jnp.arange(nblocks, dtype=jnp.int32)
    offsets = jnp.array([-1, 0, 1], dtype=jnp.int32)
    window = jnp.broadcast_to(
        (block_ids[:, None] + offsets[None, :])[None], (channel_roster, nblocks, 3)
    )
    window_ok = (window >= 0) & (window < nblocks)
    glob_slots = jnp.broadcast_to(
        anchor_tiles[:, None, :], (channel_roster, nblocks, anchor_tiles.shape[1])
    )
    glob_ok = jnp.abs(glob_slots - block_ids[None, :, None]) > 1
    rand_ok = jnp.ones(sampled_tiles.shape, dtype=bool)
    position_pointer = jnp.concatenate([window, glob_slots, sampled_tiles], axis=2)
    position_pointer = jnp.clip(position_pointer, 0, nblocks - 1)
    position_usable = jnp.concatenate([window_ok, glob_ok, rand_ok], axis=2)
    return (position_pointer, position_usable)


def share_units(device_portion, tok_local, seq_parts, copies, tile_index, tile_span):
    piece = tok_local // copies
    per_piece = piece // tile_index
    units = jnp.arange(seq_parts * per_piece, dtype=jnp.int32)
    position = (
        units // per_piece * tok_local + device_portion * piece + units % per_piece * tile_index
    )
    return position // tile_span


def attend_sample(
    probe_vector,
    matcher_tiles,
    payload_tiles,
    adjoint_signal,
    channel_scale,
    position_pointer,
    position_usable,
    tile_index,
    tile_span,
):
    q_len, channel_width = probe_vector.shape
    k_len = matcher_tiles.shape[0]
    q_units = q_len // tile_index
    k_blocks = k_len // tile_span
    group_size = group_of()
    group_count = q_units // group_size
    reciprocal_sqrt_width = 1.0 / math.sqrt(channel_width)
    key_blocks = matcher_tiles.reshape(k_blocks, tile_span, channel_width)
    value_blocks = payload_tiles.reshape(k_blocks, tile_span, channel_width)
    q_groups = probe_vector.reshape(group_count, group_size, tile_index, channel_width)
    g_groups = adjoint_signal.reshape(group_count, group_size, tile_index, channel_width)
    i_groups = position_pointer.reshape(group_count, group_size, -1)
    v_groups = position_usable.reshape(group_count, group_size, -1)

    def step(carried, inputs):
        key_acc, value_acc, temp_acc = carried
        q_blk, g_blk, idx_blk, ok_blk = inputs
        k_sel = key_blocks[idx_blk]
        v_sel = value_blocks[idx_blk]
        logit_matrix = (
            jnp.einsum("gbd,gsjd->gbsj", q_blk, k_sel, preferred_element_type=jnp.float32)
            * reciprocal_sqrt_width
        )
        position_filter = ok_blk[:, None, :, None]
        rescaled_logits = jnp.where(position_filter, channel_scale * logit_matrix, masked_minimum)
        row_max = jnp.max(rescaled_logits, axis=(2, 3), keepdims=True)
        expo_terms = jnp.where(position_filter, jnp.exp(rescaled_logits - row_max), 0.0)
        row_total = jnp.sum(expo_terms, axis=(2, 3), keepdims=True)
        attn_prob = expo_terms / row_total
        prob_low = attn_prob.astype(jnp.bfloat16)
        d_prob = jnp.einsum("gbd,gsjd->gbsj", g_blk, v_sel, preferred_element_type=jnp.float32)
        row_delta = jnp.sum(attn_prob * d_prob, axis=(2, 3), keepdims=True)
        adjoint_weights = attn_prob * (d_prob - row_delta)
        temp_acc = temp_acc + jnp.sum(adjoint_weights * logit_matrix)
        adjoint_logits = (adjoint_weights * (channel_scale * reciprocal_sqrt_width)).astype(
            jnp.bfloat16
        )
        adjoint_probe = jnp.einsum(
            "gbsj,gsjd->gbd", adjoint_logits, k_sel, preferred_element_type=jnp.float32
        )
        d_keys = jnp.einsum(
            "gbsj,gbd->gsjd", adjoint_logits, q_blk, preferred_element_type=jnp.float32
        )
        d_values = jnp.einsum("gbsj,gbd->gsjd", prob_low, g_blk, preferred_element_type=jnp.float32)
        key_acc = key_acc.at[idx_blk].add(d_keys)
        value_acc = value_acc.at[idx_blk].add(d_values)
        return ((key_acc, value_acc, temp_acc), adjoint_probe.astype(jnp.bfloat16))

    start = (
        jnp.zeros((k_blocks, tile_span, channel_width), jnp.float32),
        jnp.zeros((k_blocks, tile_span, channel_width), jnp.float32),
        jnp.zeros((), jnp.float32),
    )
    (key_acc, value_acc, temp_acc), adjoint_probe = lax.scan(
        step, start, (q_groups, g_groups, i_groups, v_groups)
    )
    return (
        adjoint_probe.reshape(q_len, channel_width),
        key_acc.reshape(k_len, channel_width).astype(jnp.bfloat16),
        value_acc.reshape(k_len, channel_width).astype(jnp.bfloat16),
        temp_acc,
    )


def on_device(
    probe_tensor,
    matcher_tensor,
    payload_tensor,
    adjoint_attended,
    logit_scale,
    anchor_tiles,
    sampled_tiles,
):
    tok_local, seq_count, width = probe_tensor.shape
    channel_roster = logit_scale.shape[0]
    channel_width = width // channel_roster
    seq_parts = lax.axis_size("seq")
    item_total = seq_count * channel_roster
    copies = max(1, seq_parts // item_total)
    per_device = max(1, item_total // seq_parts)
    piece = tok_local // copies
    tile_index = min(TILE_SPAN, piece)

    def to_samples(array):
        return jnp.repeat(array.reshape(tok_local, item_total, channel_width), copies, axis=1)

    def to_shares(array):
        split = array.reshape(copies, piece, item_total, channel_width).transpose(1, 2, 0, 3)
        return split.reshape(piece, item_total * copies, channel_width)

    query_send = to_shares(probe_tensor)
    grad_send = to_shares(adjoint_attended)
    query_item = lax.all_to_all(query_send, "seq", split_axis=1, concat_axis=0, tiled=True)
    key_item = lax.all_to_all(
        to_samples(matcher_tensor), "seq", split_axis=1, concat_axis=0, tiled=True
    )
    value_item = lax.all_to_all(
        to_samples(payload_tensor), "seq", split_axis=1, concat_axis=0, tiled=True
    )
    grad_item = lax.all_to_all(grad_send, "seq", split_axis=1, concat_axis=0, tiled=True)
    length = key_item.shape[0]
    nblocks = length // TILE_SPAN
    my_index = lax.axis_index("seq")
    replica = my_index % copies
    position_pointer, position_usable = block_lists(anchor_tiles, sampled_tiles, nblocks)
    first_item = my_index // copies * per_device
    channel_finder = (first_item + jnp.arange(per_device, dtype=jnp.int32)) % channel_roster
    channel_subset = channel_finder[:, None] == jnp.arange(channel_roster, dtype=jnp.int32)[None, :]
    sample_scales = jnp.sum(jnp.where(channel_subset, logit_scale[None, :], 0.0), axis=1)
    item_index = jnp.sum(
        jnp.where(channel_subset[:, :, None, None], position_pointer[None], 0), axis=1
    )
    item_valid = jnp.any(channel_subset[:, :, None, None] & position_usable[None], axis=1)
    tiles_per_device = share_units(replica, tok_local, seq_parts, copies, tile_index, TILE_SPAN)
    item_index = jnp.take(item_index, tiles_per_device, axis=1)
    item_valid = jnp.take(item_valid, tiles_per_device, axis=1)

    def sample_mapped(sample_operands):
        (
            probe_vector,
            matcher_tiles,
            payload_tiles,
            adjoint_signal,
            channel_scale,
            sample_indices,
            sample_valid_mask,
        ) = sample_operands
        return attend_sample(
            probe_vector,
            matcher_tiles,
            payload_tiles,
            adjoint_signal,
            channel_scale,
            sample_indices,
            sample_valid_mask,
            tile_index,
            TILE_SPAN,
        )

    adjoint_probe, adjoint_matcher, adjoint_payload, adjoint_scale = lax.map(
        sample_mapped,
        (
            jnp.moveaxis(query_item, 1, 0),
            jnp.moveaxis(key_item, 1, 0),
            jnp.moveaxis(value_item, 1, 0),
            jnp.moveaxis(grad_item, 1, 0),
            sample_scales,
            item_index,
            item_valid,
        ),
    )
    scale_pieces = jnp.sum(jnp.where(channel_subset, adjoint_scale[:, None], 0.0), axis=0)
    adjoint_scales = lax.psum(scale_pieces, ("seq", "fsdp"))
    query_grad = jnp.moveaxis(adjoint_probe, 0, 1)
    key_send = jnp.moveaxis(adjoint_matcher, 0, 1)
    value_send = jnp.moveaxis(adjoint_payload, 0, 1)
    back_query = lax.all_to_all(query_grad, "seq", split_axis=0, concat_axis=1, tiled=True)
    returned_key = lax.all_to_all(key_send, "seq", split_axis=0, concat_axis=1, tiled=True)
    returned_value = lax.all_to_all(value_send, "seq", split_axis=0, concat_axis=1, tiled=True)

    def combine_portions(received):
        summed = jnp.sum(
            received.astype(jnp.float32).reshape(tok_local, item_total, copies, channel_width),
            axis=2,
        )
        return summed.astype(jnp.bfloat16).reshape(tok_local, seq_count, width)

    query_gradients = (
        back_query.reshape(piece, item_total, copies, channel_width)
        .transpose(2, 0, 1, 3)
        .reshape(tok_local, seq_count, width)
    )
    return (
        query_gradients,
        combine_portions(returned_key),
        combine_portions(returned_value),
        adjoint_scales,
    )


def solution(mesh):
    placed = (
        P("seq", "fsdp", None),
        P("seq", "fsdp", None),
        P("seq", "fsdp", None),
        P("seq", "fsdp", None),
        P(),
        P(),
        P(),
    )
    return jax.shard_map(
        on_device,
        mesh=mesh,
        in_specs=placed,
        out_specs=(P("seq", "fsdp", None), P("seq", "fsdp", None), P("seq", "fsdp", None), P()),
        check_vma=False,
    )
```

profile of v0, /device:TPU:1, one launch (start us, length us, event | category | flops | bytes accessed | tf_op | source)
XLA Modules:
  0.0 966.9 jit_solution(14185936706878660316)
XLA Ops:
  2.8 19.5 %all-to-all-start = ((bf16[32,64,128]{2,0,1:T(8,128)(2,1)}), bf16[32,64,128]{2,0,1:T(8,128)(2,1)}, u32[]{:S(2)}, u32[]{:S(2)}) async-start(bf16[32,64,128]{2,0,1:T(8,128)(2,1)} %bitcast.24), calls=%async_computation | async-start | bytes 1048576 | tf_op jit(solution)/shard_map/all_to_all | solution.py:152
  23.5 28.3 %all-to-all-done = bf16[32,64,128]{2,0,1:T(8,128)(2,1)} async-done(((bf16[32,64,128]{2,0,1:T(8,128)(2,1)}), bf16[32,64,128]{2,0,1:T(8,128)(2,1)}, u32[]{:S(2)}, u32[]{:S(2)}) %all-to-all-start) | async-done | bytes 524320 | tf_op jit(solution)/shard_map/all_to_all | solution.py:152
  51.7 8.8 all-to-all-start.2
  60.8 29.1 %all-to-all-done.2 = bf16[32,64,128]{2,0,1:T(8,128)(2,1)} async-done(((bf16[32,64,128]{2,0,1:T(8,128)(2,1)}), bf16[32,64,128]{2,0,1:T(8,128)(2,1)}, u32[]{:S(2)}, u32[]{:S(2)}) %all-to-all-start.2) | async-done | bytes 524320 | tf_op jit(solution)/shard_map/all_to_all | solution.py:159
  91.7 8.9 all-to-all-start.1
  100.9 91.5 %all-to-all-done.1 = bf16[128,64,128]{2,0,1:T(8,128)(2,1)} async-done(((bf16[128,64,128]{2,0,1:T(8,128)(2,1)}), bf16[128,64,128]{2,0,1:T(8,128)(2,1)}, u32[]{:S(2)}, u32[]{:S(2)}) %all-to-all-start.1) | async-done | bytes 2097184 | tf_op jit(solution)/shard_map/all_to_all | solution.py:153
  194.2 14.3 %all-to-all-start.3 = ((bf16[128,64,128]{2,0,1:T(8,128)(2,1)}), bf16[128,64,128]{2,0,1:T(8,128)(2,1)}, u32[]{:S(2)}, u32[]{:S(2)}) async-start(bf16[128,64,128]{2,0,1:T(8,128)(2,1)} %bitcast.37), calls=%async_computation.3 | async-start | bytes 4194304 | tf_op jit(solution)/shard_map/all_to_all | solution.py:156
  212.1 91.3 %all-to-all-done.3 = bf16[128,64,128]{2,0,1:T(8,128)(2,1)} async-done(((bf16[128,64,128]{2,0,1:T(8,128)(2,1)}), bf16[128,64,128]{2,0,1:T(8,128)(2,1)}, u32[]{:S(2)}, u32[]{:S(2)}) %all-to-all-start.3) | async-done | bytes 2097184 | tf_op jit(solution)/shard_map/all_to_all | solution.py:156
  308.3 304.9 %while.32 = (s32[]{:T(128)}, f32[128,64,128]{2,1,0:T(8,128)}, f32[128,64,128]{2,1,0:T(8,128)}, f32[]{:T(128)}, bf16[8,8,32,128]{3,2,1,0:T(8,128)(2,1)}, /*index=...) while((s32[]{:T(128)}, f32[128,64,128]{2,1,0:T(8,128)}, ...), condition=%wide.region_10.11_spmd, body=%wide.region_3.10_spmd.sunk | while | flops 173179328 | bytes 30234488 | solution.py:113
  313.3 3.2 fusion.61
  316.5 10.3 %scatter_fusion.1 = f32[128,64,128]{2,1,0:T(8,128)} fusion(f32[128,64,128]{2,1,0:T(8,128)} %get-tuple-element.349, s32[64]{0:T(128)S(1)} %reshape.476, f32[64,64,128]{2,1,0:T(8,128)} %bitcast.170), kind=kCustom, calls=%fused_computation.5.clone.1 | custom fusion | flops 524288 | bytes 6291712 | tf_op jit(solution)/shard_map/while/body/eval_jaxpr/while/body/eval_jaxpr/scatter-add | solution.py:105
  334.8 9.0 scatter_fusion
  351.4 3.2 fusion.61
  354.6 10.3 %scatter_fusion.1 = f32[128,64,128]{2,1,0:T(8,128)} fusion(f32[128,64,128]{2,1,0:T(8,128)} %get-tuple-element.349, s32[64]{0:T(128)S(1)} %reshape.476, f32[64,64,128]{2,1,0:T(8,128)} %bitcast.170), kind=kCustom, calls=%fused_computation.5.clone.1 | custom fusion | flops 524288 | bytes 6291712 | tf_op jit(solution)/shard_map/while/body/eval_jaxpr/while/body/eval_jaxpr/scatter-add | solution.py:105
  372.9 9.1 scatter_fusion
  389.5 3.2 fusion.61
  392.7 10.4 %scatter_fusion.1 = f32[128,64,128]{2,1,0:T(8,128)} fusion(f32[128,64,128]{2,1,0:T(8,128)} %get-tuple-element.349, s32[64]{0:T(128)S(1)} %reshape.476, f32[64,64,128]{2,1,0:T(8,128)} %bitcast.170), kind=kCustom, calls=%fused_computation.5.clone.1 | custom fusion | flops 524288 | bytes 6291712 | tf_op jit(solution)/shard_map/while/body/eval_jaxpr/while/body/eval_jaxpr/scatter-add | solution.py:105
  411.0 9.0 scatter_fusion
  427.6 3.2 fusion.61
  430.8 10.4 %scatter_fusion.1 = f32[128,64,128]{2,1,0:T(8,128)} fusion(f32[128,64,128]{2,1,0:T(8,128)} %get-tuple-element.349, s32[64]{0:T(128)S(1)} %reshape.476, f32[64,64,128]{2,1,0:T(8,128)} %bitcast.170), kind=kCustom, calls=%fused_computation.5.clone.1 | custom fusion | flops 524288 | bytes 6291712 | tf_op jit(solution)/shard_map/while/body/eval_jaxpr/while/body/eval_jaxpr/scatter-add | solution.py:105
  449.1 9.0 scatter_fusion
  465.8 3.2 fusion.61
  468.9 10.4 %scatter_fusion.1 = f32[128,64,128]{2,1,0:T(8,128)} fusion(f32[128,64,128]{2,1,0:T(8,128)} %get-tuple-element.349, s32[64]{0:T(128)S(1)} %reshape.476, f32[64,64,128]{2,1,0:T(8,128)} %bitcast.170), kind=kCustom, calls=%fused_computation.5.clone.1 | custom fusion | flops 524288 | bytes 6291712 | tf_op jit(solution)/shard_map/while/body/eval_jaxpr/while/body/eval_jaxpr/scatter-add | solution.py:105
  487.3 9.1 scatter_fusion
  503.9 3.2 fusion.61
  507.1 10.3 %scatter_fusion.1 = f32[128,64,128]{2,1,0:T(8,128)} fusion(f32[128,64,128]{2,1,0:T(8,128)} %get-tuple-element.349, s32[64]{0:T(128)S(1)} %reshape.476, f32[64,64,128]{2,1,0:T(8,128)} %bitcast.170), kind=kCustom, calls=%fused_computation.5.clone.1 | custom fusion | flops 524288 | bytes 6291712 | tf_op jit(solution)/shard_map/while/body/eval_jaxpr/while/body/eval_jaxpr/scatter-add | solution.py:105
  525.4 9.0 scatter_fusion
  542.0 3.2 fusion.61
  545.1 10.3 %scatter_fusion.1 = f32[128,64,128]{2,1,0:T(8,128)} fusion(f32[128,64,128]{2,1,0:T(8,128)} %get-tuple-element.349, s32[64]{0:T(128)S(1)} %reshape.476, f32[64,64,128]{2,1,0:T(8,128)} %bitcast.170), kind=kCustom, calls=%fused_computation.5.clone.1 | custom fusion | flops 524288 | bytes 6291712 | tf_op jit(solution)/shard_map/while/body/eval_jaxpr/while/body/eval_jaxpr/scatter-add | solution.py:105
  563.4 9.0 scatter_fusion
  580.1 3.2 fusion.61
  583.2 10.4 %scatter_fusion.1 = f32[128,64,128]{2,1,0:T(8,128)} fusion(f32[128,64,128]{2,1,0:T(8,128)} %get-tuple-element.349, s32[64]{0:T(128)S(1)} %reshape.476, f32[64,64,128]{2,1,0:T(8,128)} %bitcast.170), kind=kCustom, calls=%fused_computation.5.clone.1 | custom fusion | flops 524288 | bytes 6291712 | tf_op jit(solution)/shard_map/while/body/eval_jaxpr/while/body/eval_jaxpr/scatter-add | solution.py:105
  601.5 9.1 scatter_fusion
  616.7 10.4 %all-to-all-start.4 = ((bf16[64,2,2048]{2,1,0:T(2,128)(2,1)}), bf16[64,2,2048]{2,1,0:T(2,128)(2,1)S(1)}, u32[]{:S(2)}, u32[]{:S(2)}) async-start(bf16[64,2,2048]{2,1,0:T(2,128)(2,1)} %reshape.453), calls=%async_computation.4 | async-start | bytes 1048576 | tf_op jit(solution)/shard_map/all_to_all | solution.py:216
  627.1 2.7 convert_element_type.106
  629.8 2.9 reduce.7
  632.7 4.0 reshape.455
  636.6 20.0 %all-to-all-done.4 = bf16[64,2,2048]{2,1,0:T(2,128)(2,1)S(1)} async-done(((bf16[64,2,2048]{2,1,0:T(2,128)(2,1)}), bf16[64,2,2048]{2,1,0:T(2,128)(2,1)S(1)}, u32[]{:S(2)}, u32[]{:S(2)}) %all-to-all-start.4) | async-done | bytes 524320 | tf_op jit(solution)/shard_map/all_to_all | solution.py:216
  657.4 8.8 all-to-all-start.5
  666.2 4.0 convert_element_type.114
  670.2 4.5 reduce.8
  674.7 4.0 reshape.457
  678.7 78.7 %all-to-all-done.5 = bf16[64,2,8192]{2,1,0:T(2,128)(2,1)S(1)} async-done(((bf16[64,2,8192]{2,1,0:T(2,128)(2,1)}), bf16[64,2,8192]{2,1,0:T(2,128)(2,1)S(1)}, u32[]{:S(2)}, u32[]{:S(2)}) %all-to-all-start.5) | async-done | bytes 2097184 | tf_op jit(solution)/shard_map/all_to_all | solution.py:217
  757.4 14.3 %all-to-all-start.6 = ((bf16[64,2,8192]{2,1,0:T(2,128)(2,1)}), bf16[64,2,8192]{2,1,0:T(2,128)(2,1)}, u32[]{:S(2)}, u32[]{:S(2)}) async-start(bf16[64,2,8192]{2,1,0:T(2,128)(2,1)} %reshape.457), calls=%async_computation.6 | async-start | bytes 4194304 | tf_op jit(solution)/shard_map/all_to_all | solution.py:218
  771.7 164.5 %psum.7 = f32[16]{0:T(128)} all-reduce(f32[16]{0:T(128)S(1)} %broadcast_select_fusion), channel_id=1, replica_groups=mesh['seq'=64,'fsdp'=8] {'seq','fsdp'}, use_global_device_ids=true, to_apply=%region_13.14 | all-reduce | flops 16 | bytes 128 | tf_op jit(solution)/shard_map/psum | solution.py:212
  936.2 3.6 reshape.454
  941.2 6.8 reshape.456
  952.2 10.4 %reshape.458 = bf16[8192,1,128]{2,1,0:T(2,128)(2,1)} reshape(bf16[64,2,8192]{2,1,0:T(2,128)(2,1)} %all-to-all-done.6) | data formatting | bytes 4194304
  (180 shorter events, 148.5 us)
Async XLA Ops:
  0.6 21.7 %copy-start.2 = (bf16[128,1,2048]{2,0,1:T(8,128)(2,1)S(1)}, bf16[128,1,2048]{2,0,1:T(8,128)(2,1)}, u32[]{:S(2)}) copy-start(bf16[128,1,2048]{2,0,1:T(8,128)(2,1)} %param.13) | copy-start | bytes 1572868
  2.8 48.9 %all-to-all-start = ((bf16[32,64,128]{2,0,1:T(8,128)(2,1)}), bf16[32,64,128]{2,0,1:T(8,128)(2,1)}, u32[]{:S(2)}, u32[]{:S(2)}) async-start(bf16[32,64,128]{2,0,1:T(8,128)(2,1)} %bitcast.24), calls=%async_computation | async-start | bytes 1048576 | tf_op jit(solution)/shard_map/all_to_all | solution.py:152
  22.4 38.2 %copy-start.3 = (bf16[128,1,2048]{2,0,1:T(8,128)(2,1)S(1)}, bf16[128,1,2048]{2,0,1:T(8,128)(2,1)}, u32[]{:S(2)}) copy-start(bf16[128,1,2048]{2,0,1:T(8,128)(2,1)} %param.11) | copy-start | bytes 1572868
  51.7 38.1 %all-to-all-start.2 = ((bf16[32,64,128]{2,0,1:T(8,128)(2,1)}), bf16[32,64,128]{2,0,1:T(8,128)(2,1)}, u32[]{:S(2)}, u32[]{:S(2)}) async-start(bf16[32,64,128]{2,0,1:T(8,128)(2,1)} %bitcast.33), calls=%async_computation.2 | async-start | bytes 1048576 | tf_op jit(solution)/shard_map/all_to_all | solution.py:159
  91.7 8.9 copy-start.4
  91.7 100.6 %all-to-all-start.1 = ((bf16[128,64,128]{2,0,1:T(8,128)(2,1)}), bf16[128,64,128]{2,0,1:T(8,128)(2,1)}, u32[]{:S(2)}, u32[]{:S(2)}) async-start(bf16[128,64,128]{2,0,1:T(8,128)(2,1)} %bitcast.28), calls=%async_computation.1 | async-start | bytes 4194304 | tf_op jit(solution)/shard_map/all_to_all | solution.py:153
  194.2 14.4 %copy-start.7 = (s32[3]{0:T(128)S(1)}, s32[3]{0:T(128)}, u32[]{:S(2)}) copy-start(s32[3]{0:T(128)} %constant.217.clone) | copy-start | bytes 40
  194.2 14.5 %copy-start.6 = (s32[16,2]{0,1:T(2,128)S(1)}, s32[16,2]{0,1:T(2,128)}, u32[]{:S(2)}) copy-start(s32[16,2]{0,1:T(2,128)} %param.15) | copy-start | bytes 388
  194.2 14.6 %copy-start.5 = (s32[16,128,3]{1,0,2:T(8,128)S(1)}, s32[16,128,3]{1,0,2:T(8,128)}, u32[]{:S(2)}) copy-start(s32[16,128,3]{1,0,2:T(8,128)} %param.16) | copy-start | bytes 73732
  194.2 16.5 %copy-start.8 = (f32[16]{0:T(128)S(1)}, f32[16]{0:T(128)}, u32[]{:S(2)}) copy-start(f32[16]{0:T(128)} %param.14) | copy-start | bytes 196
  194.2 109.2 %all-to-all-start.3 = ((bf16[128,64,128]{2,0,1:T(8,128)(2,1)}), bf16[128,64,128]{2,0,1:T(8,128)(2,1)}, u32[]{:S(2)}, u32[]{:S(2)}) async-start(bf16[128,64,128]{2,0,1:T(8,128)(2,1)} %bitcast.37), calls=%async_computation.3 | async-start | bytes 4194304 | tf_op jit(solution)/shard_map/all_to_all | solution.py:156
  332.6 0.8 copy-start
  370.7 0.8 copy-start
  408.9 0.8 copy-start
  447.0 0.8 copy-start
  485.1 0.8 copy-start
  523.2 0.8 copy-start
  561.3 0.8 copy-start
  599.4 0.8 copy-start
  616.7 39.9 %all-to-all-start.4 = ((bf16[64,2,2048]{2,1,0:T(2,128)(2,1)}), bf16[64,2,2048]{2,1,0:T(2,128)(2,1)S(1)}, u32[]{:S(2)}, u32[]{:S(2)}) async-start(bf16[64,2,2048]{2,1,0:T(2,128)(2,1)} %reshape.453), calls=%async_computation.4 | async-start | bytes 1048576 | tf_op jit(solution)/shard_map/all_to_all | solution.py:216
  656.6 0.8 copy-start.1
  657.4 100.0 %all-to-all-start.5 = ((bf16[64,2,8192]{2,1,0:T(2,128)(2,1)}), bf16[64,2,8192]{2,1,0:T(2,128)(2,1)S(1)}, u32[]{:S(2)}, u32[]{:S(2)}) async-start(bf16[64,2,8192]{2,1,0:T(2,128)(2,1)} %reshape.455), calls=%async_computation.5 | async-start | bytes 4194304 | tf_op jit(solution)/shard_map/all_to_all | solution.py:217
  757.4 194.8 %all-to-all-start.6 = ((bf16[64,2,8192]{2,1,0:T(2,128)(2,1)}), bf16[64,2,8192]{2,1,0:T(2,128)(2,1)}, u32[]{:S(2)}, u32[]{:S(2)}) async-start(bf16[64,2,8192]{2,1,0:T(2,128)(2,1)} %reshape.457), calls=%async_computation.6 | async-start | bytes 4194304 | tf_op jit(solution)/shard_map/all_to_all | solution.py:218
where the time goes:
time: 975 us; the launch traced here: 967 us
  waiting for transfers between devices  339 us (35%)
  other arithmetic  189 us (19%)
  blocking collectives  164 us (17%)
  local copies, waits for them, and re-layouts  98.4 us (10%)
  starting transfers between devices  85 us (9%)
  matrix products  84.5 us (9%)
    psum x1, blocking collectives, on_device(): adjoint_scales = lax.psum(scale_pieces, ('seq', 'fsdp'))  164 us
    all_to_all x1, waiting for transfers between devices, on_device(): lax.all_to_all(to_samples(matcher_tensor), 'seq', split_axis=1, concat_ax...  91.5 us
    all_to_all x1, waiting for transfers between devices, on_device(): lax.all_to_all(to_samples(payload_tensor), 'seq', split_axis=1, concat_ax...  91.3 us
    scatter-add x8, other arithmetic, step(): value_acc = value_acc.at[idx_blk].add(d_values)  82.8 us
    all_to_all x1, waiting for transfers between devices, on_device(): lax.all_to_all(key_send, 'seq', split_axis=0, concat_axis=1, tiled=True)  78.7 us
    scatter-add x8, other arithmetic, step(): key_acc = key_acc.at[idx_blk].add(d_keys)  72.3 us
    unnamed x31, local copies, waits for them, and re-layouts  39 us
    all_to_all x1, waiting for transfers between devices, on_device(): lax.all_to_all(grad_send, 'seq', split_axis=1, concat_axis=0, tiled=True)  29.1 us
  transfers between devices with their start and end apart: 7, of which 6 were waited for; matrix products, arithmetic and copies ran while one was open for 4% of the time, Pallas kernels for 0%

commit v1 on v0

v1 whole, which is shorter than its diff:
```python
import math

import jax
import jax.numpy as jnp
from jax import lax
from jax.experimental import pallas as pl
from jax.experimental.pallas import tpu as pltpu
from jax.sharding import Mesh, PartitionSpec as P

TILE = 64
WIDTH = 128
SLOTS = 8
NY = 4
TAIL = 8
MASKED = -1e30
LOG2E = 1.4426950408889634


def attend_kernel(
    y_ref, row_ref, scale_ref, bias_ref, qg_ref, own_ref, left_ref, right_ref, far0_ref, far1_ref,
    dq_ref, pown_ref, pleft_ref, pright_ref, pfar0_ref, pfar1_ref,
    kv, acc, temp, sems,
):
    pairs = qg_ref.shape[0] // (4 * TILE)
    shard = kv.shape[0] // NY
    half = shard // 2
    y_at = y_ref[0]

    def start_of(step):
        return pl.multiple_of(lax.rem(y_at + step, NY) * shard, shard)

    places = (
        (own_ref, pown_ref, start_of(0), shard),
        (left_ref, pleft_ref, start_of(3), shard),
        (right_ref, pright_ref, start_of(1), shard),
        (far0_ref, pfar0_ref, start_of(2), half),
        (far1_ref, pfar1_ref, start_of(2) + half, half),
    )
    copies = [
        pltpu.make_async_copy(source, kv.at[pl.ds(start, size), :], sems.at[n])
        for n, (source, _, start, size) in enumerate(places)
    ]
    for copy in copies:
        copy.start()

    def clear(n, carry):
        acc[pl.ds(pl.multiple_of(n * 256, 256), 256), :] = jnp.zeros((256, WIDTH), jnp.float32)
        return carry

    lax.fori_loop(0, acc.shape[0] // 256, clear, 0)
    temp[...] = jnp.zeros_like(temp)
    for copy in copies:
        copy.wait()

    inv = 1.0 / math.sqrt(WIDTH)
    coef = scale_ref[0] * inv
    coef2 = coef * LOG2E
    low_half = lax.broadcasted_iota(jnp.int32, (2 * TILE, WIDTH), 0) < TILE

    def split(x):
        zero = jnp.zeros_like(x)
        return jnp.concatenate(
            [jnp.where(low_half, x, zero), jnp.where(low_half, zero, x)], axis=1
        )

    def pair_step(p, carry):
        base = pl.multiple_of(p * 4 * TILE, 4 * TILE)
        q_diag = split(qg_ref[pl.ds(base, 2 * TILE), :])
        g_diag = split(qg_ref[pl.ds(base + 2 * TILE, 2 * TILE), :])
        at_a = [pl.multiple_of(row_ref[p * 2 * SLOTS + s], TILE) for s in range(SLOTS)]
        at_b = [pl.multiple_of(row_ref[p * 2 * SLOTS + SLOTS + s], TILE) for s in range(SLOTS)]

        def gather(shift):
            return jnp.concatenate(
                [
                    jnp.concatenate(
                        [
                            kv[pl.ds(at_a[s] + shift, TILE), :],
                            kv[pl.ds(at_b[s] + shift, TILE), :],
                        ],
                        axis=1,
                    )
                    for s in range(SLOTS)
                ],
                axis=0,
            )

        k_cat = gather(0)
        v_cat = gather(2 * TILE)
        nt = (((1,), (1,)), ((), ()))
        nn = (((1,), (0,)), ((), ()))
        tn = (((0,), (0,)), ((), ()))
        raw = lax.dot_general(k_cat, q_diag, nt, preferred_element_type=jnp.float32)
        bias = jnp.concatenate(
            [
                jnp.broadcast_to(bias_ref[p, s : s + 1, :], (TILE, 2 * TILE))
                for s in range(SLOTS)
            ],
            axis=0,
        )
        logits = raw * coef2 + bias
        top = jnp.max(logits, axis=0, keepdims=True)
        expo = jnp.exp2(logits - top)
        prob = expo * (1.0 / jnp.sum(expo, axis=0, keepdims=True))
        dprob = lax.dot_general(v_cat, g_diag, nt, preferred_element_type=jnp.float32)
        delta = jnp.sum(prob * dprob, axis=0, keepdims=True)
        dscore = prob * (dprob - delta)
        prod = dscore * raw
        temp[...] += jnp.sum(prod.reshape(SLOTS * TILE // 8, 8, 2 * TILE), axis=0)
        draw = (dscore * coef).astype(jnp.bfloat16)
        prob_low = prob.astype(jnp.bfloat16)
        dk_cat = lax.dot_general(draw, q_diag, nn, preferred_element_type=jnp.float32)
        dv_cat = lax.dot_general(prob_low, g_diag, nn, preferred_element_type=jnp.float32)
        for s in range(SLOTS):
            rows = slice(s * TILE, (s + 1) * TILE)
            for at, cols in ((at_a[s], slice(0, WIDTH)), (at_b[s], slice(WIDTH, 2 * WIDTH))):
                acc[pl.ds(at, TILE), :] += dk_cat[rows, cols]
                acc[pl.ds(at + 2 * TILE, TILE), :] += dv_cat[rows, cols]
        dq_cat = lax.dot_general(draw, k_cat, tn, preferred_element_type=jnp.float32)
        dq_ref[p, : 2 * TILE, :] = jnp.where(
            low_half, dq_cat[:, :WIDTH], dq_cat[:, WIDTH:]
        ).astype(jnp.bfloat16)
        return carry

    lax.fori_loop(0, pairs, pair_step, 0)

    total = jnp.sum(temp[...], keepdims=True) * inv
    high = total.astype(jnp.bfloat16).astype(jnp.float32)
    mid = (total - high).astype(jnp.bfloat16).astype(jnp.float32)
    low = total - high - mid
    line = lax.broadcasted_iota(jnp.int32, (TAIL, WIDTH), 0)
    tail = jnp.where(line == 0, high, jnp.where(line == 1, mid, low)).astype(jnp.bfloat16)
    for p in range(pairs):
        dq_ref[p, 2 * TILE :, :] = tail

    for _, target, start, size in places:
        def narrow(n, carry, target=target, start=start):
            at = pl.multiple_of(n * 256, 256)
            target[pl.ds(at, 256), :] = acc[pl.ds(start + at, 256), :].astype(jnp.bfloat16)
            return carry

        lax.fori_loop(0, size // 256, narrow, 0)


def local_attend(y_at, index, usable, scale, qg, own, left, right, far0, far1):
    count = index.shape[0]
    bias = jnp.where(usable, 0.0, MASKED).astype(jnp.float32)
    bias = bias.reshape(count // 2, 2, SLOTS).transpose(0, 2, 1)
    bias = jnp.repeat(bias, TILE, axis=2)
    rows = index // 2 * (4 * TILE) + index % 2 * TILE
    pairs, shard = count // 2, own.shape[0]
    vmem = pl.BlockSpec(memory_space=pltpu.VMEM)
    smem = pl.BlockSpec(memory_space=pltpu.SMEM)
    hbm = pl.BlockSpec(memory_space=pl.ANY)
    part = jax.ShapeDtypeStruct((shard, WIDTH), jnp.bfloat16)
    half = jax.ShapeDtypeStruct((shard // 2, WIDTH), jnp.bfloat16)
    return pl.pallas_call(
        attend_kernel,
        out_shape=(
            jax.ShapeDtypeStruct((pairs, 2 * TILE + TAIL, WIDTH), jnp.bfloat16),
            part, part, part, half, half,
        ),
        in_specs=[smem, smem, smem, vmem, vmem, hbm, hbm, hbm, hbm, hbm],
        out_specs=(vmem,) * 6,
        scratch_shapes=[
            pltpu.VMEM((NY * shard, WIDTH), jnp.bfloat16),
            pltpu.VMEM((NY * shard, WIDTH), jnp.float32),
            pltpu.VMEM((8, WIDTH), jnp.float32),
            pltpu.SemaphoreType.DMA((5,)),
        ],
        compiler_params=pltpu.CompilerParams(vmem_limit_bytes=48 * 1024 * 1024),
        name="attend",
    )(
        y_at.reshape(1).astype(jnp.int32), rows.reshape(-1), scale, bias, qg,
        own, left, right, far0, far1,
    )


def slot_lists(anchor_tiles, sampled_tiles, head, first, count, nblocks):
    block = first + jnp.arange(count, dtype=jnp.int32)
    window = block[:, None] + jnp.array([-1, 0, 1], dtype=jnp.int32)[None, :]
    anchors = lax.dynamic_index_in_dim(anchor_tiles, head, 0, keepdims=True)
    anchors = jnp.broadcast_to(anchors, (count, anchors.shape[1]))
    sampled = lax.dynamic_slice(
        sampled_tiles, (head, first, 0), (1, count, sampled_tiles.shape[2])
    )[0]
    index = jnp.concatenate([window, anchors, sampled], axis=1)
    usable = jnp.concatenate(
        [
            (window >= 0) & (window < nblocks),
            jnp.abs(anchors - block[:, None]) > 1,
            jnp.ones(sampled.shape, dtype=bool),
        ],
        axis=1,
    )
    return jnp.clip(index, 0, nblocks - 1), usable


def on_device(probe, matcher, payload, adjoint, logit_scale, anchor_tiles, sampled_tiles):
    tok_local, seq_count, width = probe.shape
    heads = logit_scale.shape[0]
    n_fsdp = lax.axis_size("fsdp")
    y_at, z_at = lax.axis_index("y"), lax.axis_index("z")

    def by_head(array):
        return array.reshape(tok_local, heads, WIDTH).transpose(1, 0, 2)

    def to_head(first, second):
        both = jnp.stack([by_head(first), by_head(second)], axis=1)
        return lax.all_to_all(both, "z", split_axis=0, concat_axis=0, tiled=True)

    def to_tokens(array):
        return array.transpose(1, 0, 2).reshape(tok_local, seq_count, width)

    def shift(array, step):
        return lax.ppermute(array, "y", [(n, (n + step) % NY) for n in range(NY)])

    own = to_head(matcher, payload)
    shard = own.size // WIDTH
    own = own.reshape(shard, WIDTH)
    half = shard // 2
    left = shift(own, 1)
    right = shift(own, -1)
    far0 = shift(left[:half], 1)
    far1 = shift(right[half:], -1)
    qg = to_head(probe, adjoint).reshape(shard, WIDTH)

    nblocks = NY * heads * tok_local // TILE
    count = nblocks // NY
    index, usable = slot_lists(
        anchor_tiles, sampled_tiles, z_at, y_at * count, count, nblocks
    )
    scale = lax.dynamic_slice(logit_scale, (z_at,), (1,))
    dq, pown, pleft, pright, pfar0, pfar1 = local_attend(
        y_at, index, usable, scale, qg, own, left, right, far0, far1
    )

    def add(*parts):
        total = parts[0].astype(jnp.float32)
        for other in parts[1:]:
            total = total + other.astype(jnp.float32)
        return total.astype(jnp.bfloat16)

    dq = lax.all_to_all(dq, "z", split_axis=0, concat_axis=0, tiled=True)
    from_left = shift(pfar0, 1)
    from_right = shift(pfar1, -1)
    right_sum = jnp.concatenate([add(pright[:half], from_left), pright[half:]], axis=0)
    left_sum = jnp.concatenate([pleft[:half], add(pleft[half:], from_right)], axis=0)
    mine = add(pown, shift(right_sum, 1), shift(left_sum, -1))
    mine = lax.all_to_all(
        mine.reshape(heads, 2, tok_local, WIDTH), "z", split_axis=0, concat_axis=0, tiled=True
    )

    temp = jnp.sum(dq[:, tok_local : tok_local + 3, 0].astype(jnp.float32), axis=1)
    for bit in range(n_fsdp.bit_length() - 1):
        swap = [(n, n ^ (1 << bit)) for n in range(n_fsdp)]
        temp = temp + lax.ppermute(temp, "fsdp", swap)
    for bit in range(NY.bit_length() - 1):
        swap = [(n, n ^ (1 << bit)) for n in range(NY)]
        temp = temp + lax.ppermute(temp, "y", swap)

    return to_tokens(dq[:, :tok_local]), to_tokens(mine[:, 0]), to_tokens(mine[:, 1]), temp


def solution(mesh):
    seq, fsdp = mesh.shape["seq"], mesh.shape["fsdp"]
    split_mesh = Mesh(mesh.devices.reshape(NY, seq // NY, fsdp), ("y", "z", "fsdp"))
    tokens = P(("y", "z"), "fsdp", None)
    return jax.shard_map(
        on_device,
        mesh=split_mesh,
        in_specs=(tokens, tokens, tokens, tokens, P(), P(), P()),
        out_specs=(tokens, tokens, tokens, P()),
        check_vma=False,
    )
```

time: 975 us -> 270 us (0.28)
  waiting for transfers between devices: 339 us -> 126 us
  other arithmetic: 189 us -> 6.88 us
  blocking collectives: 164 us -> 0 us
  matrix products: 84.5 us -> 0 us
  local copies, waits for them, and re-layouts: 98.4 us -> 19.1 us
  Pallas kernels: 0 us -> 18.9 us
    all_to_all x7 -> x4, waiting for transfers between devices: 339 us -> 64.8 us  [the longest x2 49.8 us: to_head(): return lax.all_to_all(both, 'z', split_axis=0, concat_axis=0, tiled=True)]
    psum x1 -> x0, blocking collectives: 164 us -> none  [on_device(): adjoint_scales = lax.psum(scale_pieces, ('seq', 'fsdp'))]
    scatter-add x16 -> x0, other arithmetic: 155 us -> none  [the longest x8 82.8 us: step(): value_acc = value_acc.at[idx_blk].add(d_values)]
    dot_general x40 -> x0, matrix products: 84.5 us -> none  [the longest x8 25.2 us: step(): jnp.einsum('gbsj,gbd->gsjd', prob_low, g_blk, preferred_element_type=jnp....]
    ppermute x0 -> x13, waiting for transfers between devices: none -> 60.7 us  [the longest x8 52.6 us: shift(): return lax.ppermute(array, 'y', [(n, (n + step) % NY) for n in range(NY)])]
    ppermute x0 -> x13, starting transfers between devices: none -> 41.6 us  [the longest x8 24.1 us: shift(): return lax.ppermute(array, 'y', [(n, (n + step) % NY) for n in range(NY)])]
    gather x18 -> x0, local copies, waits for them, and re-layouts: 38.7 us -> none  [the longest x8 18.7 us: step(): k_sel = key_blocks[idx_blk]]
    all_to_all x7 -> x4, starting transfers between devices: 85 us -> 52.1 us  [the longest x2 28.9 us: to_head(): return lax.all_to_all(both, 'z', split_axis=0, concat_axis=0, tiled=True)]
  transfers between devices with their start and end apart: 7 -> 17, of which waited for: 6 -> 13; matrix products, arithmetic and copies ran while one was open for 4% -> 5% of each run, Pallas kernels for 0% -> 0%
where the time goes in v1:
time: 270 us; the launch traced here: 265 us
  waiting for transfers between devices  126 us (47%)
  starting transfers between devices  93.8 us (35%)
  local copies, waits for them, and re-layouts  19.1 us (7%)
  Pallas kernels  18.9 us (7%)
  other arithmetic  6.88 us (3%)
    ppermute x8, waiting for transfers between devices, shift(): return lax.ppermute(array, 'y', [(n, (n + step) % NY) for n in range(NY)])  52.6 us
    all_to_all x2, waiting for transfers between devices, to_head(): return lax.all_to_all(both, 'z', split_axis=0, concat_axis=0, tiled=True)  49.8 us
    all_to_all x2, starting transfers between devices, to_head(): return lax.all_to_all(both, 'z', split_axis=0, concat_axis=0, tiled=True)  28.9 us
    ppermute x8, starting transfers between devices, shift(): return lax.ppermute(array, 'y', [(n, (n + step) % NY) for n in range(NY)])  24.1 us
    pallas_call x1, Pallas kernels, local_attend(): pl.pallas_call(attend_kernel, out_shape=(jax.ShapeDtypeStruct((pairs, 2 *...  18.9 us
    all_to_all x1, waiting for transfers between devices, on_device(): lax.all_to_all(mine.reshape(heads, 2, tok_local, WIDTH), 'z', split_axis=...  15 us
    ppermute x3, starting transfers between devices, on_device(): temp = temp + lax.ppermute(temp, 'fsdp', swap)  13.7 us
    all_to_all x1, starting transfers between devices, on_device(): dq = lax.all_to_all(dq, 'z', split_axis=0, concat_axis=0, tiled=True)  12.4 us
  transfers between devices with their start and end apart: 17, of which 13 were waited for; matrix products, arithmetic and copies ran while one was open for 5% of the time, Pallas kernels for 0%

profile of v1, /device:TPU:1, one launch (start us, length us, event | category | flops | bytes accessed | tf_op | source)
XLA Modules:
  0.0 265.1 jit_solution(3881570937328492515)
XLA Ops:
  0.7 1.2 copy.40
  2.3 1.0 pad_maximum_fusion.1
  3.3 15.9 %all-to-all-start.1 = ((bf16[16,2,128,128]{3,2,1,0:T(8,128)(2,1)}), bf16[16,2,128,128]{3,2,1,0:T(8,128)(2,1)S(1)}, u32[]{:S(2)}, u32[]{:S(2)}) async-start(bf16[16,2,128,128]{3,2,1,0:T(8,128)(2,1)} %pad_maximum_fusion.1), calls=%async_computation.1 | async-start | bytes 2097152 | tf_op jit(solution)/shard_map/all_to_all | solution.py:210
  19.3 0.9 copy-done.13
  20.6 1.1 pad_maximum_fusion
  21.7 42.5 %all-to-all-done.1 = bf16[16,2,128,128]{3,2,1,0:T(8,128)(2,1)S(1)} async-done(((bf16[16,2,128,128]{3,2,1,0:T(8,128)(2,1)}), bf16[16,2,128,128]{3,2,1,0:T(8,128)(2,1)S(1)}, u32[]{:S(2)}, u32[]{:S(2)}) %all-to-all-start.1) | async-done | bytes 1048608 | tf_op jit(solution)/shard_map/all_to_all | solution.py:210
  64.2 13.0 %all-to-all-start = ((bf16[16,2,128,128]{3,2,1,0:T(8,128)(2,1)}), bf16[16,2,128,128]{3,2,1,0:T(8,128)(2,1)S(1)}, u32[]{:S(2)}, u32[]{:S(2)}) async-start(bf16[16,2,128,128]{3,2,1,0:T(8,128)(2,1)} %pad_maximum_fusion), calls=%async_computation | async-start | bytes 2097152 | tf_op jit(solution)/shard_map/all_to_all | solution.py:210
  77.2 4.6 %collective-permute-start.1 = (bf16[4096,128]{1,0:T(8,128)(2,1)S(1)}, bf16[4096,128]{1,0:T(8,128)(2,1)S(1)}, u32[]{:S(2)}, u32[]{:S(2)}) collective-permute-start(bf16[4096,128]{1,0:T(8,128)(2,1)S(1)} %bitcast.52), channel_id=1, source_target_pairs={{0,384},{128,0},{256,128},{384,256},{1,385},{129,1},{257,129},{385... | collective-permute-start | bytes 3145736 | tf_op jit(solution)/shard_map/ppermute | solution.py:216
  81.9 1.9 collective-permute-start
  84.4 19.2 %collective-permute-done.1.right_ref = bf16[4096,128]{1,0:T(8,128)(2,1)S(1)} collective-permute-done((bf16[4096,128]{1,0:T(8,128)(2,1)S(1)}, bf16[4096,128]{1,0:T(8,128)(2,1)S(1)}, u32[]{:S(2)}, u32[]{:S(2)}) %collective-permute-start.1) | collective-permute-done | bytes 1048608 | tf_op jit(solution)/shard_map/ppermute | solution.py:216
  103.6 1.0 copy-done.10
  104.6 0.8 slice.41
  105.4 5.3 %collective-permute-start.3 = (bf16[2048,128]{1,0:T(8,128)(2,1)}, bf16[2048,128]{1,0:T(8,128)(2,1)S(1)}, u32[]{:S(2)}, u32[]{:S(2)}) collective-permute-start(bf16[2048,128]{1,0:T(8,128)(2,1)} %slice.41), channel_id=1, source_target_pairs={{0,384},{128,0},{256,128},{384,256},{1,385},{129,1},{257,129},{385... | collective-permute-start | bytes 1572872 | tf_op jit(solution)/shard_map/ppermute | solution.py:216
  110.7 1.1 slice.40
  111.8 1.9 collective-permute-start.2
  115.2 7.3 %all-to-all-done = bf16[16,2,128,128]{3,2,1,0:T(8,128)(2,1)S(1)} async-done(((bf16[16,2,128,128]{3,2,1,0:T(8,128)(2,1)}), bf16[16,2,128,128]{3,2,1,0:T(8,128)(2,1)S(1)}, u32[]{:S(2)}, u32[]{:S(2)}) %all-to-all-start) | async-done | bytes 1048608 | tf_op jit(solution)/shard_map/all_to_all | solution.py:210
  122.5 0.8 copy-done.2
  123.4 3.1 %collective-permute-done.2.far0_ref = bf16[2048,128]{1,0:T(8,128)(2,1)S(1)} collective-permute-done((bf16[2048,128]{1,0:T(8,128)(2,1)S(1)}, bf16[2048,128]{1,0:T(8,128)(2,1)S(1)}, u32[]{:S(2)}, u32[]{:S(2)}) %collective-permute-start.2) | collective-permute-done | bytes 524320 | tf_op jit(solution)/shard_map/ppermute | solution.py:216
  127.3 1.0 copy-done.3
  128.3 1.0 copy-done.5
  129.4 18.9 %attend.1 = (bf16[16,136,128]{2,1,0:T(8,128)(2,1)S(1)}, bf16[4096,128]{1,0:T(8,128)(2,1)S(1)}, bf16[4096,128]{1,0:T(8,128)(2,1)S(1)}, bf16[4096,128]{1,0:T(8,128...) custom-call(s32[1]{0:T(128)} %bitcast.y_ref, s32[256]{0:T(256)S(1)} %fusion.2.row_ref, ...), custom_call_target="tpu_custom_call" | custom-call | tf_op jit(solution)/shard_map/attend/pallas_call | solution.py:157
  148.3 0.8 copy-done.1
  149.9 1.9 collective-permute-start.6
  151.8 12.4 %all-to-all-start.2 = ((bf16[16,136,128]{2,1,0:T(8,128)(2,1)}), bf16[16,136,128]{2,1,0:T(8,128)(2,1)}, u32[]{:S(2)}, u32[]{:S(2)}) async-start(bf16[16,136,128]{2,1,0:T(8,128)(2,1)} %copy-done.1), calls=%async_computation.2 | async-start | bytes 1114112 | tf_op jit(solution)/shard_map/all_to_all | solution.py:244
  164.3 0.9 copy-done.7
  165.2 1.9 collective-permute-start.4
  167.2 1.2 add_convert_fusion.1
  168.4 4.6 %collective-permute-start.7 = (bf16[4096,128]{1,0:T(8,128)(2,1)S(1)}, bf16[4096,128]{1,0:T(8,128)(2,1)S(1)}, u32[]{:S(2)}, u32[]{:S(2)}) collective-permute-start(bf16[4096,128]{1,0:T(8,128)(2,1)S(1)} %pad_maximum_fusion.3), channel_id=1, source_target_pairs={{0,384},{128,0},{256,128},{384,256},{1,385},{129,1},{257,129},{385... | collective-permute-start | bytes 3145736 | tf_op jit(solution)/shard_map/ppermute | solution.py:216
  173.0 7.0 %collective-permute-done.4 = bf16[2048,128]{1,0:T(8,128)(2,1)S(1)} collective-permute-done((bf16[2048,128]{1,0:T(8,128)(2,1)S(1)}, bf16[2048,128]{1,0:T(8,128)(2,1)S(1)}, u32[]{:S(2)}, u32[]{:S(2)}) %collective-permute-start.4) | collective-permute-done | bytes 524320 | tf_op jit(solution)/shard_map/ppermute | solution.py:216
  180.2 1.9 collective-permute-start.5
  182.2 11.2 %collective-permute-done.7 = bf16[4096,128]{1,0:T(8,128)(2,1)S(1)} collective-permute-done((bf16[4096,128]{1,0:T(8,128)(2,1)S(1)}, bf16[4096,128]{1,0:T(8,128)(2,1)S(1)}, u32[]{:S(2)}, u32[]{:S(2)}) %collective-permute-start.7) | collective-permute-done | bytes 1048608 | tf_op jit(solution)/shard_map/ppermute | solution.py:216
  193.3 12.1 %collective-permute-done.5 = bf16[4096,128]{1,0:T(8,128)(2,1)S(1)} collective-permute-done((bf16[4096,128]{1,0:T(8,128)(2,1)S(1)}, bf16[4096,128]{1,0:T(8,128)(2,1)S(1)}, u32[]{:S(2)}, u32[]{:S(2)}) %collective-permute-start.5) | collective-permute-done | bytes 1048608 | tf_op jit(solution)/shard_map/ppermute | solution.py:216
  205.4 1.4 add_convert_fusion
  206.8 10.9 %all-to-all-start.3 = ((bf16[16,2,128,128]{3,2,1,0:T(8,128)(2,1)}), bf16[16,2,128,128]{3,2,1,0:T(8,128)(2,1)S(1)}, u32[]{:S(2)}, u32[]{:S(2)}) async-start(bf16[16,2,128,128]{3,2,1,0:T(8,128)(2,1)} %bitcast.14), calls=%async_computation.3 | async-start | bytes 2097152 | tf_op jit(solution)/shard_map/all_to_all | solution.py:250
  217.7 1.0 convert_reduce_fusion
  218.6 6.0 %collective-permute-start.8 = (f32[16]{0:T(128)S(1)}, f32[16]{0:T(128)S(1)}, u32[]{:S(2)}, u32[]{:S(2)}) collective-permute-start(f32[16]{0:T(128)S(1)} %convert_reduce_fusion), channel_id=1, source_target_pairs={{0,1},{1,0},{2,3},{3,2},{4,5},{5,4},{6,7},{7,6},{8,9},{9,8},{10,11... | collective-permute-start | bytes 200 | tf_op jit(solution)/shard_map/ppermute | solution.py:257
  225.4 3.1 %collective-permute-start.9 = (f32[16]{0:T(128)S(1)}, f32[16]{0:T(128)S(1)}, u32[]{:S(2)}, u32[]{:S(2)}) collective-permute-start(f32[16]{0:T(128)S(1)} %add.103), channel_id=1, source_target_pairs={{0,2},{1,3},{2,0},{3,1},{4,6},{5,7},{6,4},{7,5},{8,10},{9,11},{10,... | collective-permute-start | bytes 200 | tf_op jit(solution)/shard_map/ppermute | solution.py:257
  228.5 1.5 collective-permute-done.9
  230.0 4.7 %collective-permute-start.10 = (f32[16]{0:T(128)S(1)}, f32[16]{0:T(128)S(1)}, u32[]{:S(2)}, u32[]{:S(2)}) collective-permute-start(f32[16]{0:T(128)S(1)} %add.104), channel_id=1, source_target_pairs={{0,4},{1,5},{2,6},{3,7},{4,0},{5,1},{6,2},{7,3},{8,12},{9,13},{10,... | collective-permute-start | bytes 200 | tf_op jit(solution)/shard_map/ppermute | solution.py:257
  234.7 1.1 slice_bitcast_fusion.2
  236.1 1.9 collective-permute-start.11
  238.3 2.4 collective-permute-done.11
  240.7 1.9 collective-permute-start.12
  242.6 1.0 copy.36
  243.6 3.2 %collective-permute-done.12 = f32[16]{0:T(128)S(1)} collective-permute-done((f32[16]{0:T(128)S(1)}, f32[16]{0:T(128)S(1)}, u32[]{:S(2)}, u32[]{:S(2)}) %collective-permute-start.12) | collective-permute-done | bytes 96 | tf_op jit(solution)/shard_map/ppermute | solution.py:260
  247.3 15.0 %all-to-all-done.3 = bf16[16,2,128,128]{3,2,1,0:T(8,128)(2,1)S(1)} async-done(((bf16[16,2,128,128]{3,2,1,0:T(8,128)(2,1)}), bf16[16,2,128,128]{3,2,1,0:T(8,128)(2,1)S(1)}, u32[]{:S(2)}, u32[]{:S(2)}) %all-to-all-start.3) | async-done | bytes 1048608 | tf_op jit(solution)/shard_map/all_to_all | solution.py:250
  262.8 1.0 reshape.88
  264.1 1.0 reshape.87
  (72 shorter events, 7.7 us)
Async XLA Ops:
  0.6 83.4 %copy-start = (s32[16,128,3]{1,0,2:T(8,128)S(1)}, s32[16,128,3]{1,0,2:T(8,128)}, u32[]{:S(2)}) copy-start(s32[16,128,3]{1,0,2:T(8,128)} %param.14) | copy-start | bytes 73732
  0.6 1.2 copy-start.11
  3.3 15.9 %copy-start.12 = (bf16[128,1,2048]{2,0,1:T(8,128)(2,1)S(1)}, bf16[128,1,2048]{2,0,1:T(8,128)(2,1)}, u32[]{:S(2)}) copy-start(bf16[128,1,2048]{2,0,1:T(8,128)(2,1)} %param.8) | copy-start | bytes 1572868
  3.3 60.9 %all-to-all-start.1 = ((bf16[16,2,128,128]{3,2,1,0:T(8,128)(2,1)}), bf16[16,2,128,128]{3,2,1,0:T(8,128)(2,1)S(1)}, u32[]{:S(2)}, u32[]{:S(2)}) async-start(bf16[16,2,128,128]{3,2,1,0:T(8,128)(2,1)} %pad_maximum_fusion.1), calls=%async_computation.1 | async-start | bytes 2097152 | tf_op jit(solution)/shard_map/all_to_all | solution.py:210
  19.2 1.0 copy-start.13
  21.7 62.1 %copy-start.15 = (s32[16,2]{0,1:T(2,128)S(1)}, s32[16,2]{0,1:T(2,128)}, u32[]{:S(2)}) copy-start(s32[16,2]{0,1:T(2,128)} %param.13) | copy-start | bytes 388
  21.7 62.6 %copy-start.14 = (s32[3]{0:T(128)S(1)}, s32[3]{0:T(128)}, u32[]{:S(2)}) copy-start(s32[3]{0:T(128)} %constant.66.clone) | copy-start | bytes 40
  64.2 17.7 %copy-start.8 = (bf16[16,2,128,128]{3,2,1,0:T(8,128)(2,1)}, bf16[16,2,128,128]{3,2,1,0:T(8,128)(2,1)S(1)}, u32[]{:S(2)}) copy-start(bf16[16,2,128,128]{3,2,1,0:T(8,128)(2,1)S(1)} %all-to-all-done.1) | copy-start | bytes 3145732
  64.2 58.3 %all-to-all-start = ((bf16[16,2,128,128]{3,2,1,0:T(8,128)(2,1)}), bf16[16,2,128,128]{3,2,1,0:T(8,128)(2,1)S(1)}, u32[]{:S(2)}, u32[]{:S(2)}) async-start(bf16[16,2,128,128]{3,2,1,0:T(8,128)(2,1)} %pad_maximum_fusion), calls=%async_computation | async-start | bytes 2097152 | tf_op jit(solution)/shard_map/all_to_all | solution.py:210
  77.2 26.4 %collective-permute-start.1 = (bf16[4096,128]{1,0:T(8,128)(2,1)S(1)}, bf16[4096,128]{1,0:T(8,128)(2,1)S(1)}, u32[]{:S(2)}, u32[]{:S(2)}) collective-permute-start(bf16[4096,128]{1,0:T(8,128)(2,1)S(1)} %bitcast.52), channel_id=1, source_target_pairs={{0,384},{128,0},{256,128},{384,256},{1,385},{129,1},{257,129},{385... | collective-permute-start | bytes 3145736 | tf_op jit(solution)/shard_map/ppermute | solution.py:216
  81.9 28.8 %collective-permute-start = (bf16[4096,128]{1,0:T(8,128)(2,1)S(1)}, bf16[4096,128]{1,0:T(8,128)(2,1)}, u32[]{:S(2)}, u32[]{:S(2)}) collective-permute-start(bf16[4096,128]{1,0:T(8,128)(2,1)S(1)} %bitcast.53), channel_id=1, source_target_pairs={{0,128},{128,256},{256,384},{384,0},{1,129},{129,257},{257,385},{3... | collective-permute-start | bytes 3145736 | tf_op jit(solution)/shard_map/ppermute | solution.py:216
  84.4 29.4 %copy-start.16 = (f32[16]{0:T(128)S(1)}, f32[16]{0:T(128)}, u32[]{:S(2)}) copy-start(f32[16]{0:T(128)} %param.12) | copy-start | bytes 196
  103.6 1.0 copy-start.10
  105.4 17.1 %collective-permute-start.3 = (bf16[2048,128]{1,0:T(8,128)(2,1)}, bf16[2048,128]{1,0:T(8,128)(2,1)S(1)}, u32[]{:S(2)}, u32[]{:S(2)}) collective-permute-start(bf16[2048,128]{1,0:T(8,128)(2,1)} %slice.41), channel_id=1, source_target_pairs={{0,384},{128,0},{256,128},{384,256},{1,385},{129,1},{257,129},{385... | collective-permute-start | bytes 1572872 | tf_op jit(solution)/shard_map/ppermute | solution.py:216
  111.8 14.7 %collective-permute-start.2 = (bf16[2048,128]{1,0:T(8,128)(2,1)S(1)}, bf16[2048,128]{1,0:T(8,128)(2,1)S(1)}, u32[]{:S(2)}, u32[]{:S(2)}) collective-permute-start(bf16[2048,128]{1,0:T(8,128)(2,1)S(1)} %slice.40), channel_id=1, source_target_pairs={{0,128},{128,256},{256,384},{384,0},{1,129},{129,257},{257,385},{3... | collective-permute-start | bytes 1572872 | tf_op jit(solution)/shard_map/ppermute | solution.py:216
  122.5 4.8 %copy-start.9 = (bf16[16,2,128,128]{3,2,1,0:T(8,128)(2,1)}, bf16[16,2,128,128]{3,2,1,0:T(8,128)(2,1)S(1)}, u32[]{:S(2)}) copy-start(bf16[16,2,128,128]{3,2,1,0:T(8,128)(2,1)S(1)} %all-to-all-done) | copy-start | bytes 3145732
  122.5 0.8 copy-start.2
  126.5 0.8 copy-start.4
  127.3 1.0 copy-start.3
  128.3 1.0 copy-start.5
  148.3 0.8 copy-start.1
  149.1 0.8 copy-start.6
  149.9 17.3 %collective-permute-start.6 = (bf16[2048,128]{1,0:T(8,128)(2,1)}, bf16[2048,128]{1,0:T(8,128)(2,1)}, u32[]{:S(2)}, u32[]{:S(2)}) collective-permute-start(bf16[2048,128]{1,0:T(8,128)(2,1)} %get-tuple-element.15), channel_id=1, source_target_pairs={{0,384},{128,0},{256,128},{384,256},{1,385},{129,1},{257,129},{385... | collective-permute-start | bytes 1572872 | tf_op jit(solution)/shard_map/ppermute | solution.py:216
  151.8 55.0 %all-to-all-start.2 = ((bf16[16,136,128]{2,1,0:T(8,128)(2,1)}), bf16[16,136,128]{2,1,0:T(8,128)(2,1)}, u32[]{:S(2)}, u32[]{:S(2)}) async-start(bf16[16,136,128]{2,1,0:T(8,128)(2,1)} %copy-done.1), calls=%async_computation.2 | async-start | bytes 1114112 | tf_op jit(solution)/shard_map/all_to_all | solution.py:244
  164.2 1.0 copy-start.7
  165.2 14.8 %collective-permute-start.4 = (bf16[2048,128]{1,0:T(8,128)(2,1)S(1)}, bf16[2048,128]{1,0:T(8,128)(2,1)S(1)}, u32[]{:S(2)}, u32[]{:S(2)}) collective-permute-start(bf16[2048,128]{1,0:T(8,128)(2,1)S(1)} %copy-done.7), channel_id=1, source_target_pairs={{0,128},{128,256},{256,384},{384,0},{1,129},{129,257},{257,385},{3... | collective-permute-start | bytes 1572872 | tf_op jit(solution)/shard_map/ppermute | solution.py:216
  168.4 24.9 %collective-permute-start.7 = (bf16[4096,128]{1,0:T(8,128)(2,1)S(1)}, bf16[4096,128]{1,0:T(8,128)(2,1)S(1)}, u32[]{:S(2)}, u32[]{:S(2)}) collective-permute-start(bf16[4096,128]{1,0:T(8,128)(2,1)S(1)} %pad_maximum_fusion.3), channel_id=1, source_target_pairs={{0,384},{128,0},{256,128},{384,256},{1,385},{129,1},{257,129},{385... | collective-permute-start | bytes 3145736 | tf_op jit(solution)/shard_map/ppermute | solution.py:216
  180.2 25.2 %collective-permute-start.5 = (bf16[4096,128]{1,0:T(8,128)(2,1)S(1)}, bf16[4096,128]{1,0:T(8,128)(2,1)S(1)}, u32[]{:S(2)}, u32[]{:S(2)}) collective-permute-start(bf16[4096,128]{1,0:T(8,128)(2,1)S(1)} %pad_maximum_fusion.2), channel_id=1, source_target_pairs={{0,128},{128,256},{256,384},{384,0},{1,129},{129,257},{257,385},{3... | collective-permute-start | bytes 3145736 | tf_op jit(solution)/shard_map/ppermute | solution.py:216
  206.8 55.5 %all-to-all-start.3 = ((bf16[16,2,128,128]{3,2,1,0:T(8,128)(2,1)}), bf16[16,2,128,128]{3,2,1,0:T(8,128)(2,1)S(1)}, u32[]{:S(2)}, u32[]{:S(2)}) async-start(bf16[16,2,128,128]{3,2,1,0:T(8,128)(2,1)} %bitcast.14), calls=%async_computation.3 | async-start | bytes 2097152 | tf_op jit(solution)/shard_map/all_to_all | solution.py:250
  218.6 6.8 %collective-permute-start.8 = (f32[16]{0:T(128)S(1)}, f32[16]{0:T(128)S(1)}, u32[]{:S(2)}, u32[]{:S(2)}) collective-permute-start(f32[16]{0:T(128)S(1)} %convert_reduce_fusion), channel_id=1, source_target_pairs={{0,1},{1,0},{2,3},{3,2},{4,5},{5,4},{6,7},{7,6},{8,9},{9,8},{10,11... | collective-permute-start | bytes 200 | tf_op jit(solution)/shard_map/ppermute | solution.py:257
  225.4 4.6 %collective-permute-start.9 = (f32[16]{0:T(128)S(1)}, f32[16]{0:T(128)S(1)}, u32[]{:S(2)}, u32[]{:S(2)}) collective-permute-start(f32[16]{0:T(128)S(1)} %add.103), channel_id=1, source_target_pairs={{0,2},{1,3},{2,0},{3,1},{4,6},{5,7},{6,4},{7,5},{8,10},{9,11},{10,... | collective-permute-start | bytes 200 | tf_op jit(solution)/shard_map/ppermute | solution.py:257
  230.0 6.1 %collective-permute-start.10 = (f32[16]{0:T(128)S(1)}, f32[16]{0:T(128)S(1)}, u32[]{:S(2)}, u32[]{:S(2)}) collective-permute-start(f32[16]{0:T(128)S(1)} %add.104), channel_id=1, source_target_pairs={{0,4},{1,5},{2,6},{3,7},{4,0},{5,1},{6,2},{7,3},{8,12},{9,13},{10,... | collective-permute-start | bytes 200 | tf_op jit(solution)/shard_map/ppermute | solution.py:257
  236.1 4.6 %collective-permute-start.11 = (f32[16]{0:T(128)S(1)}, f32[16]{0:T(128)S(1)}, u32[]{:S(2)}, u32[]{:S(2)}) collective-permute-start(f32[16]{0:T(128)S(1)} %add.105), channel_id=1, source_target_pairs={{0,128},{128,0},{256,384},{384,256},{1,129},{129,1},{257,385},{385... | collective-permute-start | bytes 200 | tf_op jit(solution)/shard_map/ppermute | solution.py:260
  240.7 6.1 %collective-permute-start.12 = (f32[16]{0:T(128)S(1)}, f32[16]{0:T(128)S(1)}, u32[]{:S(2)}, u32[]{:S(2)}) collective-permute-start(f32[16]{0:T(128)S(1)} %add.106), channel_id=1, source_target_pairs={{0,256},{128,384},{256,0},{384,128},{1,257},{129,385},{257,1},{385... | collective-permute-start | bytes 200 | tf_op jit(solution)/shard_map/ppermute | solution.py:260
